TPU v7x, 256 devices: a whole 4x4x8 slice. The times are simulated.
256 devices in a mesh: wide: 64 (over y, z, core), narrow: 4 (over x).
Axes of the slice: x: 4, y: 4, z: 8, core: 2. Of those that a mesh axis runs over, the one named last changes fastest.
Arguments:
- residual_in: bfloat16 [128, 7168], P('wide', 'narrow'), may hold values from -2 to 2
- query_nope: bfloat16 [128, 64, 128], P('wide', 'narrow'), may hold values from -6 to 6
- query_rope: bfloat16 [128, 64, 64], P('wide', 'narrow'), may hold values from -8 to 8
- absorb_key: bfloat16 [64, 128, 512], P('narrow'), may hold values from -0.5 to 0.5
- absorb_value: bfloat16 [64, 512, 128], P('narrow'), may hold values from -0.25 to 0.25
- latent_cache: bfloat16 [128, 2048, 576], P('wide'), may hold values from -8 to 8
- cache_lengths: int32 [128], P('wide'), may hold values from 256 to 2048, as said below
- slot_rows: int32 [128], replicated, may hold values from 0 to 127, each once
- out_proj: bfloat16 [8192, 7168], P('wide', 'narrow'), may hold values from -0.0625 to 0.0625
- norm_gain: bfloat16 [7168], P('narrow'), may hold values from 0.25 to 1.75
- gate_weight: bfloat16 [7168, 18432], P('narrow', 'wide'), may hold values from -0.0625 to 0.0625
- up_weight: bfloat16 [7168, 18432], P('narrow', 'wide'), may hold values from -0.0625 to 0.0625
- down_weight: bfloat16 [18432, 7168], P('wide', 'narrow'), may hold values from -0.046875 to 0.046875
Outputs:
- residual_out: bfloat16 [128, 7168], P('wide', 'narrow')
Inputs may be any that keep to these rules, and one draw needn't show every extreme that they name: `cache_lengths`: every slot has at least 256 live positions; in every draw some slot is full. `slot_rows`: each batch row is named by exactly one slot.
All inputs are finite; a program needn't handle non-finite values.
Results may differ from a plain program's by a relative error of at most 0.009.
Values may be sent and summed in bfloat16 or wider, within the bound.
A program may use at most 64 MiB of HBM per device.

v0:
```python
import math
import jax
import jax.numpy as jnp
from jax import lax
from jax.sharding import PartitionSpec as P

D = 7168


def shards(
    residual_in,
    query_nope,
    query_rope,
    absorb_key,
    absorb_value,
    latent_cache,
    cache_lengths,
    slot_rows,
    out_proj,
    norm_gain,
    gate_weight,
    up_weight,
    down_weight,
):
    slot_count = latent_cache.shape[0]
    head_size = query_nope.shape[2]
    latent_width = absorb_key.shape[2]
    group_index = lax.axis_index("wide")
    packed_queries = jnp.concatenate([query_nope, query_rope], axis=2)
    gathered = lax.all_gather(packed_queries, "wide", axis=0, tiled=True)
    my_rows = lax.dynamic_slice_in_dim(slot_rows, group_index * slot_count, slot_count)
    selected = jnp.take(gathered, my_rows, axis=0)
    query_latent = jnp.einsum(
        "rhd,hdc->rhc", selected[:, :, :head_size], absorb_key, preferred_element_type=jnp.float32
    ).astype(jnp.bfloat16)
    full_query = jnp.concatenate([query_latent, selected[:, :, head_size:]], axis=2)
    scale = 1.0 / math.sqrt(full_query.shape[2] - latent_width + head_size)
    scores = (
        jnp.einsum("rhc,rtc->rht", full_query, latent_cache, preferred_element_type=jnp.float32)
        * scale
    )
    positions = jnp.arange(latent_cache.shape[1], dtype=jnp.int32)
    live = positions[None, None, :] < cache_lengths[:, None, None]
    scores = jnp.where(live, scores, -jnp.inf)
    highest = jnp.max(scores, axis=2, keepdims=True)
    weights = jnp.where(live, jnp.exp(scores - highest), 0.0)
    probs = (weights / jnp.sum(weights, axis=2, keepdims=True)).astype(jnp.bfloat16)
    context = jnp.einsum("rht,rtc->rhc", probs, latent_cache, preferred_element_type=jnp.float32)
    context = context[:, :, :latent_width].astype(jnp.bfloat16)
    heads_out = jnp.einsum(
        "rhc,hcd->rhd", context, absorb_value, preferred_element_type=jnp.float32
    ).astype(jnp.bfloat16)
    every_head = lax.all_gather(heads_out, "narrow", axis=1, tiled=True)
    flat_heads = every_head.reshape(slot_count, -1)
    head_columns = lax.all_to_all(flat_heads, "wide", split_axis=1, concat_axis=0, tiled=True)
    inverse = jnp.argsort(slot_rows)
    attention = lax.psum_scatter(
        jnp.dot(
            jnp.take(head_columns, inverse, axis=0), out_proj, preferred_element_type=jnp.float32
        ),
        "wide",
        scatter_dimension=0,
        tiled=True,
    )
    middle = residual_in.astype(jnp.float32) + attention
    square_sum = lax.psum(jnp.sum(middle * middle, axis=1), "narrow")
    normed = (
        middle * lax.rsqrt(square_sum / D + 1e-06)[:, None] * norm_gain.astype(jnp.float32)
    ).astype(jnp.bfloat16)
    hidden_cols = gate_weight.shape[1]
    row_piece = lax.all_gather(normed, "wide", axis=0, tiled=True)
    local_terms = jnp.concatenate(
        [
            jnp.dot(row_piece, gate_weight, preferred_element_type=jnp.float32),
            jnp.dot(row_piece, up_weight, preferred_element_type=jnp.float32),
        ],
        axis=1,
    )
    summed = lax.psum(local_terms, "narrow")
    hidden = (jax.nn.silu(summed[:, :hidden_cols]) * summed[:, hidden_cols:]).astype(jnp.bfloat16)
    ffn_total = lax.psum_scatter(
        jnp.dot(hidden, down_weight, preferred_element_type=jnp.float32),
        "wide",
        scatter_dimension=0,
        tiled=True,
    )
    return (middle + ffn_total).astype(jnp.bfloat16)


def solution(mesh):
    in_specs = (
        P("wide", "narrow"),
        P("wide", "narrow", None),
        P("wide", "narrow", None),
        P("narrow", None, None),
        P("narrow", None, None),
        P("wide", None, None),
        P("wide"),
        P(),
        P("wide", "narrow"),
        P("narrow"),
        P("narrow", "wide"),
        P("narrow", "wide"),
        P("wide", "narrow"),
    )
    out_specs = P("wide", "narrow")
    return jax.shard_map(shards, mesh=mesh, in_specs=in_specs, out_specs=out_specs, check_vma=False)
```

profile of v0, /device:TPU:2, one launch (start us, length us, event | category | flops | bytes accessed | tf_op | source)
XLA Modules:
  0.0 592.2 jit_solution(973563443931683544)
XLA Ops:
  6.5 0.9 compare_and_fusion
  7.4 0.7 pad_maximum_fusion.1
  8.2 53.8 %all_gather.9 = bf16[128,16,192]{2,1,0:T(8,128)(2,1)S(1)} all-gather(bf16[2,16,192]{2,1,0:T(8,128)(2,1)S(1)} %pad_maximum_fusion.1), channel_id=1, replica_groups=mesh['wide'=64,'narrow'=4] {'wide'}, dimensions={0}, use_global_device_ids=true | all-gather | bytes 798720 | tf_op jit(solution)/shard_map/all_gather | solution.py:30
  62.6 0.7 iota_compare_fusion
  63.7 3.1 fusion.4
  67.0 3.7 fusion.7
  70.8 2.0 fusion.5
  72.8 12.7 %all_gather.10 = bf16[2,64,128]{2,0,1:T(2,128)(2,1)} all-gather(bf16[2,16,128]{2,0,1:T(2,128)(2,1)S(1)} %fusion.5), channel_id=1, replica_groups=mesh['wide'=64,'narrow'=4] {'narrow'}, dimensions={1}, use_global_device_ids=true | all-gather | bytes 40960 | tf_op jit(solution)/shard_map/all_gather | solution.py:53
  85.6 6.7 %all-to-all-start = ((bf16[2,64,128]{2,0,1:T(2,128)(2,1)}), bf16[2,64,128]{2,0,1:T(2,128)(2,1)S(1)}, u32[]{:S(2)}, u32[]{:S(2)}) async-start(bf16[2,64,128]{2,0,1:T(2,128)(2,1)} %all_gather.10), calls=%async_computation | async-start | bytes 65536 | tf_op jit(solution)/shard_map/all_to_all | solution.py:55
  92.4 2.5 sort.17
  94.9 6.9 %all-to-all-done = bf16[2,64,128]{2,0,1:T(2,128)(2,1)S(1)} async-done(((bf16[2,64,128]{2,0,1:T(2,128)(2,1)}), bf16[2,64,128]{2,0,1:T(2,128)(2,1)S(1)}, u32[]{:S(2)}, u32[]{:S(2)}) %all-to-all-start) | async-done | bytes 32800 | tf_op jit(solution)/shard_map/all_to_all | solution.py:55
  102.6 1.3 fusion.16
  105.2 180.9 %all-reduce.8.cloned.1.call-done = f32[128,1792]{1,0:T(8,128)} async-done(((f32[128,1792]{1,0:T(8,128)}), f32[128,1792]{1,0:T(8,128)}) %all-reduce.8.cloned.1.call-update) | async-done | bytes 917520
  286.1 1.0 multiply_reduce_fusion
  287.0 8.6 %psum.14 = f32[2]{0:T(128)S(1)} all-reduce(f32[2]{0:T(128)S(1)} %multiply_reduce_fusion), channel_id=1, replica_groups=mesh['wide'=64,'narrow'=4] {'narrow'}, use_global_device_ids=true, to_apply=%region_5.6 | all-reduce | flops 2 | bytes 16 | tf_op jit(solution)/shard_map/psum | solution.py:66
  295.6 0.9 fusion.23
  296.5 48.1 %all-gather = bf16[64,2,1792]{2,1,0:T(2,128)(2,1)S(1)} all-gather(bf16[1,2,1792]{2,1,0:T(2,128)(2,1)S(1)} %fusion.23), channel_id=1, replica_groups=mesh['wide'=64,'narrow'=4] {'wide'}, dimensions={0}, use_global_device_ids=true | all-gather | bytes 465920 | tf_op jit(solution)/shard_map/all_gather | solution.py:71
  344.8 1.6 fusion.31
  346.5 1.6 fusion.30
  348.1 0.7 pad_maximum_fusion
  349.0 42.7 %all-reduce.6.cloned.1.call-done = f32[128,576]{0,1:T(8,128)} async-done(((f32[128,576]{0,1:T(8,128)}), f32[128,576]{0,1:T(8,128)}) %all-reduce.6.cloned.1.call-update) | async-done | bytes 294928 | tf_op jit(solution)/shard_map/psum | solution.py:79
  391.7 2.8 fusion.9
  394.5 189.7 %all-reduce.10.cloned.1.call-done = f32[128,1792]{1,0:T(8,128)} async-done(((f32[128,1792]{1,0:T(8,128)}), f32[128,1792]{1,0:T(8,128)}) %all-reduce.10.cloned.1.call-update) | async-done | bytes 917520
  584.2 1.5 fusion.20
  (36 shorter events, 3.0 us)
Async XLA Ops:
  6.5 56.8 %copy-start = (bf16[16,128,512]{2,1,0:T(8,128)(2,1)S(1)}, bf16[16,128,512]{2,1,0:T(8,128)(2,1)}, u32[]{:S(2)}) copy-start(bf16[16,128,512]{2,1,0:T(8,128)(2,1)} %param.16) | copy-start | bytes 6291460
  70.8 21.6 %copy-start.4 = (s32[128]{0:T(128)S(1)}, s32[128]{0:T(128)}, u32[]{:S(2)}) copy-start(s32[128]{0:T(128)} %param.20) | copy-start | bytes 1540
  70.8 31.8 %copy-start.1 = (bf16[128,1792]{1,0:T(8,128)(2,1)S(1)}, bf16[128,1792]{1,0:T(8,128)(2,1)}, u32[]{:S(2)}) copy-start(bf16[128,1792]{1,0:T(8,128)(2,1)} %param.21) | copy-start | bytes 1376260
  70.8 33.2 %copy-start.5 = (u32[256]{0:T(256)S(1)}, u32[256]{0:T(256)}, u32[]{:S(2)}) copy-start(u32[256]{0:T(256)} %constant.62) | copy-start | bytes 3076
  70.8 215.3 %copy-start.2 = (bf16[2,1792]{1,0:T(2,128)(2,1)S(1)}, bf16[2,1792]{1,0:T(2,128)(2,1)}, u32[]{:S(2)}) copy-start(bf16[2,1792]{1,0:T(2,128)(2,1)} %param.13) | copy-start | bytes 21508
  70.8 216.2 %copy-start.3 = (bf16[1792]{0:T(1024)(128)(2,1)S(1)}, bf16[1792]{0:T(1024)(128)(2,1)}, u32[]{:S(2)}) copy-start(bf16[1792]{0:T(1024)(128)(2,1)} %param.22) | copy-start | bytes 10756
  85.6 16.3 %all-to-all-start = ((bf16[2,64,128]{2,0,1:T(2,128)(2,1)}), bf16[2,64,128]{2,0,1:T(2,128)(2,1)S(1)}, u32[]{:S(2)}, u32[]{:S(2)}) async-start(bf16[2,64,128]{2,0,1:T(2,128)(2,1)} %all_gather.10), calls=%async_computation | async-start | bytes 65536 | tf_op jit(solution)/shard_map/all_to_all | solution.py:55
  92.3 193.7 %all-reduce.8.cloned.1.call-start = ((), (), s32[]{:S(2)}) async-start(), calls=%async_computation.2 | async-start | bytes 1835008
  103.9 287.8 %all-reduce.6.cloned.1.call-start = ((), (), s32[]{:S(2)}) async-start(), calls=%async_computation.1 | async-start | bytes 589824 | tf_op jit(solution)/shard_map/psum | solution.py:79
  348.9 235.3 %all-reduce.10.cloned.1.call-start = ((), (), s32[]{:S(2)}) async-start(), calls=%async_computation.3 | async-start | bytes 1835008
Sparse Core Ops, SparseCore 0:
  104.0 182.0 all-reduce.7
  349.0 42.5 all-reduce.5
  395.1 189.0 all-reduce.9
where the time goes:
time: 593 us; the launch traced here: 592 us
  waiting for transfers between devices  420 us (71%)
  blocking collectives  123 us (21%)
  matrix products  16.6 us (3%)
  between operations  13.9 us (2%)
  other arithmetic  9.27 us (2%)
  starting transfers between devices  6.87 us (1%)
    unnamed x5, waiting for transfers between devices  371 us
    all_gather x1, blocking collectives, shards(): gathered = lax.all_gather(packed_queries, 'wide', axis=0, tiled=True)  53.8 us
    all_gather x1, blocking collectives, shards(): row_piece = lax.all_gather(normed, 'wide', axis=0, tiled=True)  48.1 us
    psum x1, waiting for transfers between devices, shards(): summed = lax.psum(local_terms, 'narrow')  42.7 us
    all_gather x1, blocking collectives, shards(): every_head = lax.all_gather(heads_out, 'narrow', axis=1, tiled=True)  12.7 us
  transfers between devices with their start and end apart: 4, of which 4 were waited for; matrix products, arithmetic and copies ran while one was open for 1% of the time, Pallas kernels for 0%

commit v1 on v0

--- a/solution.py
+++ b/solution.py
@@ -76,7 +76,9 @@
         ],
         axis=1,
     )
-    summed = lax.psum(local_terms, "narrow")
+    summed = local_terms
+    for hop in (1, 2):
+        summed = summed + lax.ppermute(summed, "narrow", [(dev, dev ^ hop) for dev in range(4)])
     hidden = (jax.nn.silu(summed[:, :hidden_cols]) * summed[:, hidden_cols:]).astype(jnp.bfloat16)
     ffn_total = lax.psum_scatter(
         jnp.dot(hidden, down_weight, preferred_element_type=jnp.float32),

time: 593 us -> 562 us (0.948)
  waiting for transfers between devices: 420 us -> 389 us
    psum x1 -> x0, waiting for transfers between devices: 42.7 us -> none  [shards(): summed = lax.psum(local_terms, 'narrow')]
    ppermute x0 -> x2, waiting for transfers between devices: none -> 17.4 us  [shards(): lax.ppermute(summed, 'narrow', [(dev, dev ^ hop) for dev in range(4)])]
    unnamed x5 -> x4, waiting for transfers between devices: 371 us -> 364 us
  transfers between devices with their start and end apart: 4 -> 5, of which waited for: 4 -> 5; matrix products, arithmetic and copies ran while one was open for 1% -> 1% of each run, Pallas kernels for 0% -> 0%
where the time goes in v1:
time: 562 us
  waiting for transfers between devices  389 us (69%)
  blocking collectives  123 us (22%)
  matrix products  15.3 us (3%)
  between operations  14.2 us (3%)
  starting transfers between devices  9.71 us (2%)
  other arithmetic  8.6 us (2%)
    unnamed x4, waiting for transfers between devices  364 us
    all_gather x1, blocking collectives, shards(): gathered = lax.all_gather(packed_queries, 'wide', axis=0, tiled=True)  53.8 us
    all_gather x1, blocking collectives, shards(): row_piece = lax.all_gather(normed, 'wide', axis=0, tiled=True)  48.1 us
    ppermute x2, waiting for transfers between devices, shards(): lax.ppermute(summed, 'narrow', [(dev, dev ^ hop) for dev in range(4)])  17.4 us
    all_gather x1, blocking collectives, shards(): every_head = lax.all_gather(heads_out, 'narrow', axis=1, tiled=True)  12.7 us
  transfers between devices with their start and end apart: 5, of which 5 were waited for; matrix products, arithmetic and copies ran while one was open for 1% of the time, Pallas kernels for 0%

profile of v1, /device:TPU:2, one launch (start us, length us, event | category | flops | bytes accessed | tf_op | source)
XLA Modules:
  0.0 561.8 jit_solution(1390198431209638278)
XLA Ops:
  6.5 0.9 compare_and_fusion
  8.2 53.8 %all_gather.9 = bf16[128,16,192]{2,1,0:T(8,128)(2,1)S(1)} all-gather(bf16[2,16,192]{2,1,0:T(8,128)(2,1)S(1)} %pad_maximum_fusion.1), channel_id=1, replica_groups=mesh['wide'=64,'narrow'=4] {'wide'}, dimensions={0}, use_global_device_ids=true | all-gather | bytes 798720 | tf_op jit(solution)/shard_map/all_gather | solution.py:30
  62.6 0.7 iota_compare_fusion
  63.7 3.1 fusion.4
  67.0 3.7 fusion.7
  70.8 2.0 fusion.5
  72.8 12.7 %all_gather.10 = bf16[2,64,128]{2,0,1:T(2,128)(2,1)} all-gather(bf16[2,16,128]{2,0,1:T(2,128)(2,1)S(1)} %fusion.5), channel_id=1, replica_groups=mesh['wide'=64,'narrow'=4] {'narrow'}, dimensions={1}, use_global_device_ids=true | all-gather | bytes 40960 | tf_op jit(solution)/shard_map/all_gather | solution.py:53
  85.6 6.7 %all-to-all-start = ((bf16[2,64,128]{2,0,1:T(2,128)(2,1)}), bf16[2,64,128]{2,0,1:T(2,128)(2,1)S(1)}, u32[]{:S(2)}, u32[]{:S(2)}) async-start(bf16[2,64,128]{2,0,1:T(2,128)(2,1)} %all_gather.10), calls=%async_computation | async-start | bytes 65536 | tf_op jit(solution)/shard_map/all_to_all | solution.py:55
  92.4 2.5 sort.17
  94.9 6.9 %all-to-all-done = bf16[2,64,128]{2,0,1:T(2,128)(2,1)S(1)} async-done(((bf16[2,64,128]{2,0,1:T(2,128)(2,1)}), bf16[2,64,128]{2,0,1:T(2,128)(2,1)S(1)}, u32[]{:S(2)}, u32[]{:S(2)}) %all-to-all-start) | async-done | bytes 32800 | tf_op jit(solution)/shard_map/all_to_all | solution.py:55
  102.6 1.3 fusion.16
  105.2 180.9 %all-reduce.5.cloned.1.call-done = f32[128,1792]{1,0:T(8,128)} async-done(((f32[128,1792]{1,0:T(8,128)}), f32[128,1792]{1,0:T(8,128)}) %all-reduce.5.cloned.1.call-update) | async-done | bytes 917520
  286.1 1.0 multiply_reduce_fusion
  287.0 8.6 %psum.7 = f32[2]{0:T(128)S(1)} all-reduce(f32[2]{0:T(128)S(1)} %multiply_reduce_fusion), channel_id=1, replica_groups=mesh['wide'=64,'narrow'=4] {'narrow'}, use_global_device_ids=true, to_apply=%region_5.6 | all-reduce | flops 2 | bytes 16 | tf_op jit(solution)/shard_map/psum | solution.py:66
  295.6 0.9 fusion.23
  296.5 48.1 %all-gather = bf16[64,2,1792]{2,1,0:T(2,128)(2,1)S(1)} all-gather(bf16[1,2,1792]{2,1,0:T(2,128)(2,1)S(1)} %fusion.23), channel_id=1, replica_groups=mesh['wide'=64,'narrow'=4] {'wide'}, dimensions={0}, use_global_device_ids=true | all-gather | bytes 465920 | tf_op jit(solution)/shard_map/all_gather | solution.py:71
  344.8 1.6 fusion.32
  346.5 1.7 fusion.31
  348.3 2.5 collective-permute-start
  350.7 7.5 %collective-permute-done = f32[128,576]{0,1:T(8,128)S(1)} collective-permute-done((f32[128,576]{0,1:T(8,128)S(1)}, f32[128,576]{0,1:T(8,128)S(1)}, u32[]{:S(2)}, u32[]{:S(2)}) %collective-permute-start) | collective-permute-done | bytes 294944 | tf_op jit(solution)/shard_map/ppermute | solution.py:81
  358.7 9.9 %collective-permute-done.1 = f32[128,576]{0,1:T(8,128)S(1)} collective-permute-done((f32[128,576]{0,1:T(8,128)S(1)}, f32[128,576]{0,1:T(8,128)S(1)}, u32[]{:S(2)}, u32[]{:S(2)}) %collective-permute-start.1) | collective-permute-done | bytes 294944 | tf_op jit(solution)/shard_map/ppermute | solution.py:81
  368.6 1.4 fusion.9
  370.0 183.5 %all-reduce.7.cloned.1.call-done = f32[128,1792]{1,0:T(8,128)} async-done(((f32[128,1792]{1,0:T(8,128)}), f32[128,1792]{1,0:T(8,128)}) %all-reduce.7.cloned.1.call-update) | async-done | bytes 917520
  553.5 1.5 fusion.20
  (41 shorter events, 4.1 us)
Async XLA Ops:
  6.5 56.8 %copy-start = (bf16[16,128,512]{2,1,0:T(8,128)(2,1)S(1)}, bf16[16,128,512]{2,1,0:T(8,128)(2,1)}, u32[]{:S(2)}) copy-start(bf16[16,128,512]{2,1,0:T(8,128)(2,1)} %param.16) | copy-start | bytes 6291460
  70.8 21.6 %copy-start.5 = (s32[128]{0:T(128)S(1)}, s32[128]{0:T(128)}, u32[]{:S(2)}) copy-start(s32[128]{0:T(128)} %param.20) | copy-start | bytes 1540
  70.8 31.8 %copy-start.2 = (bf16[128,1792]{1,0:T(8,128)(2,1)S(1)}, bf16[128,1792]{1,0:T(8,128)(2,1)}, u32[]{:S(2)}) copy-start(bf16[128,1792]{1,0:T(8,128)(2,1)} %param.21) | copy-start | bytes 1376260
  70.8 33.2 %copy-start.6 = (u32[256]{0:T(256)S(1)}, u32[256]{0:T(256)}, u32[]{:S(2)}) copy-start(u32[256]{0:T(256)} %constant.62) | copy-start | bytes 3076
  70.8 215.3 %copy-start.3 = (bf16[2,1792]{1,0:T(2,128)(2,1)S(1)}, bf16[2,1792]{1,0:T(2,128)(2,1)}, u32[]{:S(2)}) copy-start(bf16[2,1792]{1,0:T(2,128)(2,1)} %param.13) | copy-start | bytes 21508
  70.8 216.2 %copy-start.4 = (bf16[1792]{0:T(1024)(128)(2,1)S(1)}, bf16[1792]{0:T(1024)(128)(2,1)}, u32[]{:S(2)}) copy-start(bf16[1792]{0:T(1024)(128)(2,1)} %param.22) | copy-start | bytes 10756
  85.6 16.3 %all-to-all-start = ((bf16[2,64,128]{2,0,1:T(2,128)(2,1)}), bf16[2,64,128]{2,0,1:T(2,128)(2,1)S(1)}, u32[]{:S(2)}, u32[]{:S(2)}) async-start(bf16[2,64,128]{2,0,1:T(2,128)(2,1)} %all_gather.10), calls=%async_computation | async-start | bytes 65536 | tf_op jit(solution)/shard_map/all_to_all | solution.py:55
  92.3 193.7 %all-reduce.5.cloned.1.call-start = ((), (), s32[]{:S(2)}) async-start(), calls=%async_computation.1 | async-start | bytes 1835008
  103.9 449.6 %all-reduce.7.cloned.1.call-start = ((), (), s32[]{:S(2)}) async-start(), calls=%async_computation.2 | async-start | bytes 1835008
  346.5 22.1 %copy-start.1 = (bf16[288,1792]{1,0:T(8,128)(2,1)S(1)}, bf16[288,1792]{1,0:T(8,128)(2,1)}, u32[]{:S(2)}) copy-start(bf16[288,1792]{1,0:T(8,128)(2,1)} %param.25) | copy-start | bytes 3096580
  348.3 10.0 %collective-permute-start = (f32[128,576]{0,1:T(8,128)S(1)}, f32[128,576]{0,1:T(8,128)S(1)}, u32[]{:S(2)}, u32[]{:S(2)}) collective-permute-start(f32[128,576]{0,1:T(8,128)S(1)} %pad_maximum_fusion), channel_id=1, source_target_pairs={{0,1},{1,0},{2,3},{3,2},{4,5},{5,4},{6,7},{7,6},{8,9},{9,8},{10,11... | collective-permute-start | bytes 884744 | tf_op jit(solution)/shard_map/ppermute | solution.py:81
  358.3 10.3 %collective-permute-start.1 = (f32[128,576]{0,1:T(8,128)S(1)}, f32[128,576]{0,1:T(8,128)S(1)}, u32[]{:S(2)}, u32[]{:S(2)}) collective-permute-start(f32[128,576]{0,1:T(8,128)S(1)} %fusion.29), channel_id=1, source_target_pairs={{0,2},{1,3},{2,0},{3,1},{4,6},{5,7},{6,4},{7,5},{8,10},{9,11},{10,... | collective-permute-start | bytes 884744 | tf_op jit(solution)/shard_map/ppermute | solution.py:81
Sparse Core Ops, SparseCore 0:
  104.0 182.0 all-reduce.4
  370.2 183.3 all-reduce.6
